TPU v7x, 256 devices: a whole 4x4x8 slice. The times are simulated.
256 devices in a mesh: dp: 16 (over x, y), head: 16 (over z, core).
Axes of the slice: x: 4, y: 4, z: 8, core: 2. Of those that a mesh axis runs over, the one named last changes fastest.
Arguments:
- query: bfloat16 [32768, 12288], P(('dp', 'head')), may hold values from -160 to 160
- latent: bfloat16 [32768, 576], P(('dp', 'head')), may hold values from -6 to 6
- d_attn: bfloat16 [32768, 8192], P(('dp', 'head')), may hold values from -6 to 6
- w_kv: bfloat16 [512, 16384], P('dp', 'head'), may hold values from -0.25 to 0.25
- doc_lengths: int32 [16, 10], P('dp'), may hold values from 1 to 384, 2048 in all within a row
Outputs:
- d_query: bfloat16 [32768, 12288], P(('dp', 'head'))
- d_latent: float32 [32768, 576], P(('dp', 'head'))
- d_w_kv: float32 [512, 16384], P('dp', 'head')
Inputs may be any that keep to these rules, and one draw needn't show every extreme that they name: `doc_lengths`: row g lists the lengths of the 10 documents of data group g; they sum to 2048, and the longest of each row is exactly 384.
All inputs are finite; a program needn't handle non-finite values.
Results may differ from a plain program's by a relative error of at most 0.025.
Values may be sent and summed in bfloat16 or wider, within the bound.
No kernel may reach another device: no remote copies, remote signals or barrier semaphores. Data moves between devices by JAX's collectives and lax.ppermute only.
A program may use at most 128 MiB of HBM per device.

v0:
```python
import math
import jax
import jax.numpy as jnp
from jax import lax
from jax.sharding import PartitionSpec as P

NOPE = 128
ROPE = 64
VDIM = 128
KV_RANK = 512
DOC_MAX = 384
QB = 128
masked_score = -1e30


def document_index(lengths_row, count):
    ends = jnp.cumsum(lengths_row)
    positions = jnp.arange(count, dtype=jnp.int32)
    return jnp.sum((positions[:, None] >= ends[None, :]).astype(jnp.int32), axis=1)


def attend_backward(queries, keys_padded, values_padded, grads_out, doc_padded, block, window):
    seq_len = queries.shape[0]
    reach = window - block
    scale = 1.0 / math.sqrt(queries.shape[2])
    blocks = seq_len // block

    def one_block(carry, index):
        grad_keys, grad_values = carry
        first = index * block
        query_rows = lax.dynamic_slice_in_dim(queries, first, block, 0)
        key_rows = lax.dynamic_slice_in_dim(keys_padded, first, window, 0)
        value_rows = lax.dynamic_slice_in_dim(values_padded, first, window, 0)
        out_rows = lax.dynamic_slice_in_dim(grads_out, first, block, 0)
        query_doc = lax.dynamic_slice_in_dim(doc_padded, first + reach, block, 0)
        key_doc = lax.dynamic_slice_in_dim(doc_padded, first, window, 0)
        query_pos = jnp.arange(block, dtype=jnp.int32) + reach
        key_pos = jnp.arange(window, dtype=jnp.int32)
        allowed = (key_pos[None, :] <= query_pos[:, None]) & (
            key_doc[None, :] == query_doc[:, None]
        )
        scores = (
            jnp.einsum("qhd,khd->hqk", query_rows, key_rows, preferred_element_type=jnp.float32)
            * scale
        )
        scores = jnp.where(allowed[None], scores, masked_score)
        top = jnp.max(scores, axis=2, keepdims=True)
        weights = jnp.exp(scores - top)
        probs = weights / jnp.sum(weights, axis=2, keepdims=True)
        probs_low = probs.astype(jnp.bfloat16)
        attn_out = jnp.einsum(
            "hqk,khd->qhd", probs_low, value_rows, preferred_element_type=jnp.float32
        )
        delta = jnp.sum(out_rows.astype(jnp.float32) * attn_out, axis=2)
        dprob = jnp.einsum("qhd,khd->hqk", out_rows, value_rows, preferred_element_type=jnp.float32)
        dscore_low = (probs * (dprob - jnp.transpose(delta)[:, :, None])).astype(jnp.bfloat16)
        grad_query = (
            jnp.einsum("hqk,khd->qhd", dscore_low, key_rows, preferred_element_type=jnp.float32)
            * scale
        )
        grad_key_rows = (
            jnp.einsum("hqk,qhd->khd", dscore_low, query_rows, preferred_element_type=jnp.float32)
            * scale
        )
        grad_value_rows = jnp.einsum(
            "hqk,qhd->khd", probs_low, out_rows, preferred_element_type=jnp.float32
        )
        grad_keys = lax.dynamic_update_slice_in_dim(
            grad_keys,
            lax.dynamic_slice_in_dim(grad_keys, first, window, 0) + grad_key_rows,
            first,
            0,
        )
        grad_values = lax.dynamic_update_slice_in_dim(
            grad_values,
            lax.dynamic_slice_in_dim(grad_values, first, window, 0) + grad_value_rows,
            first,
            0,
        )
        return ((grad_keys, grad_values), grad_query.astype(jnp.bfloat16))

    start_keys = jnp.zeros(keys_padded.shape, jnp.float32)
    start_values = jnp.zeros(values_padded.shape, jnp.float32)
    (grad_keys, grad_values), grad_queries = lax.scan(
        one_block, (start_keys, start_values), jnp.arange(blocks, dtype=jnp.int32)
    )
    grad_queries = grad_queries.reshape(seq_len, queries.shape[1] * queries.shape[2])
    return (grad_keys[reach:], grad_values[reach:], grad_queries)


def local(query, latent, d_attn, w_kv, doc_lengths):
    group_size = lax.axis_size("head")
    own_tokens = query.shape[0]
    seq_len = own_tokens * group_size
    head_count = w_kv.shape[1] // (NOPE + VDIM)
    queries, grads_out = (
        lax.all_to_all(query, "head", split_axis=1, concat_axis=0, tiled=True),
        lax.all_to_all(d_attn, "head", split_axis=1, concat_axis=0, tiled=True),
    )
    latents = lax.all_gather(latent, "head", axis=0, tiled=True)
    compressed = latents[:, :KV_RANK]
    whole_weight = lax.all_gather(w_kv, "dp", axis=0, tiled=True)
    kv_up = jnp.dot(compressed, whole_weight, preferred_element_type=jnp.float32)
    kv_up = kv_up.astype(jnp.bfloat16).reshape(seq_len, head_count, NOPE + VDIM)
    rotary = jnp.broadcast_to(latents[:, None, KV_RANK:], (seq_len, head_count, ROPE))
    keys = jnp.concatenate([kv_up[:, :, :NOPE], rotary], axis=2)
    keys_padded = jnp.concatenate(
        [jnp.zeros((DOC_MAX, head_count, NOPE + ROPE), jnp.bfloat16), keys], axis=0
    )
    values_padded = jnp.concatenate(
        [jnp.zeros((DOC_MAX, head_count, VDIM), jnp.bfloat16), kv_up[:, :, NOPE:]], axis=0
    )
    doc_ids = document_index(doc_lengths[0], seq_len)
    doc_padded = jnp.concatenate([jnp.full((DOC_MAX,), -1, jnp.int32), doc_ids])
    grad_keys, grad_values, grad_queries = attend_backward(
        queries.reshape(seq_len, head_count, NOPE + ROPE),
        keys_padded,
        values_padded,
        grads_out.reshape(seq_len, head_count, VDIM),
        doc_padded,
        QB,
        DOC_MAX + QB,
    )
    returned = lax.all_to_all(grad_queries, "head", split_axis=0, concat_axis=1, tiled=True)
    grad_kv = jnp.concatenate([grad_keys[:, :, :NOPE], grad_values], axis=2).astype(jnp.bfloat16)
    grad_kv = grad_kv.reshape(seq_len, head_count * (NOPE + VDIM))
    grad_weight = lax.psum_scatter(
        lax.dot_general(
            compressed, grad_kv, (((0,), (0,)), ((), ())), preferred_element_type=jnp.float32
        ).astype(jnp.bfloat16),
        "dp",
        scatter_dimension=0,
        tiled=True,
    ).astype(jnp.float32)
    grad_compressed = lax.dot_general(
        grad_kv, whole_weight, (((1,), (1,)), ((), ())), preferred_element_type=jnp.float32
    )
    head_terms = jnp.concatenate([grad_compressed, jnp.sum(grad_keys[:, :, NOPE:], axis=1)], axis=1)
    summed = lax.psum(head_terms.astype(jnp.bfloat16), "head").astype(jnp.float32)
    grad_latent = lax.dynamic_slice_in_dim(
        summed, lax.axis_index("head") * own_tokens, own_tokens, 0
    )
    return (returned, grad_latent, grad_weight)


def solution(mesh):
    placed = (
        P(("dp", "head"), None),
        P(("dp", "head"), None),
        P(("dp", "head"), None),
        P("dp", "head"),
        P("dp", None),
    )
    return jax.shard_map(
        local,
        mesh=mesh,
        in_specs=placed,
        out_specs=(P(("dp", "head"), None), P(("dp", "head"), None), P("dp", "head")),
        check_vma=False,
    )
```

profile of v0, /device:TPU:2, one launch (start us, length us, event | category | flops | bytes accessed | tf_op | source)
XLA Modules:
  0.0 728.3 jit_solution(18205139117940249030)
XLA Ops:
  7.2 4.1 copy.52
  11.2 8.6 %all-to-all-start.1 = ((bf16[128,16,512]{0,2,1:T(8,128)(2,1)}), bf16[128,16,512]{0,2,1:T(8,128)(2,1)S(1)}, u32[]{:S(2)}, u32[]{:S(2)}) async-start(bf16[128,16,512]{0,2,1:T(8,128)(2,1)} %bitcast.74), calls=%async_computation.1 | async-start | bytes 4194304 | tf_op jit(solution)/shard_map/all_to_all | solution.py:98
  21.3 4.6 copy.50
  25.9 43.1 %all-to-all-done.1 = bf16[128,16,512]{0,2,1:T(8,128)(2,1)S(1)} async-done(((bf16[128,16,512]{0,2,1:T(8,128)(2,1)}), bf16[128,16,512]{0,2,1:T(8,128)(2,1)S(1)}, u32[]{:S(2)}, u32[]{:S(2)}) %all-to-all-start.1) | async-done | bytes 2097184 | tf_op jit(solution)/shard_map/all_to_all | solution.py:98
  70.4 4.7 all-to-all-start
  75.4 4.3 copy.53
  79.7 4.2 reshape.117
  83.9 74.2 %all-gather.3.cloned.1.call-done = bf16[2048,576]{0,1:T(8,128)(2,1)} async-done(((bf16[128,576]{0,1:T(8,128)(2,1)}), bf16[2048,576]{0,1:T(8,128)(2,1)}) %all-gather.3.cloned.1.call-update) | async-done | bytes 2359312 | tf_op jit(solution)/shard_map/all_gather | solution.py:100
  158.1 4.2 convolution_convert_fusion
  165.0 4.0 copy.66
  168.9 3.4 concatenate.23
  174.4 3.7 copy.51
  178.1 5.8 reshape.113
  183.9 3.5 broadcast_in_dim.54
  190.0 266.0 %while.16 = (s32[]{:T(128)}, f32[2432,4,192]{0,2,1:T(8,128)}, f32[2432,4,128]{0,2,1:T(8,128)}, bf16[16,128,4,192]{1,3,2,0:T(8,128)(2,1)}, s32[16]{0:T(128)S(1)},...) while((s32[]{:T(128)}, f32[2432,4,192]{0,2,1:T(8,128)}, ...), condition=%wide.region_6.7_spmd, body=%wide.region_2.6_spmd.sunk | while | flops 711002240 | bytes 15294786 | solution.py:84
  198.0 3.1 fusion.127
  201.1 3.3 fusion.128
  214.7 3.2 fusion.127
  217.8 3.3 fusion.128
  231.3 3.1 fusion.127
  234.4 3.3 fusion.128
  251.0 3.3 fusion.128
  264.5 3.1 fusion.127
  267.7 3.3 fusion.128
  281.2 3.1 fusion.127
  284.3 3.3 fusion.128
  300.9 3.3 fusion.128
  317.5 3.3 fusion.128
  334.1 3.3 fusion.128
  347.6 3.1 fusion.127
  350.7 3.3 fusion.128
  364.3 3.1 fusion.127
  367.3 3.3 fusion.128
  380.8 3.1 fusion.127
  384.0 3.3 fusion.128
  397.5 3.1 fusion.127
  400.6 3.3 fusion.128
  414.1 3.1 fusion.127
  417.2 3.3 fusion.128
  433.8 3.3 fusion.128
  447.4 3.1 fusion.127
  450.5 3.3 fusion.128
  455.9 4.7 copy.56
  460.6 6.1 all-to-all-start.2
  479.1 6.3 fusion.67
  487.7 142.7 %all-reduce.5.cloned.1.call-done = bf16[2048,576]{0,1:T(8,128)(2,1)} async-done(((bf16[2048,576]{0,1:T(8,128)(2,1)}), bf16[2048,576]{0,1:T(8,128)(2,1)}) %all-reduce.5.cloned.1.call-update) | async-done | bytes 2359312 | tf_op jit(solution)/shard_map/psum | solution.py:139
  632.0 80.5 %reduce-scatter.4.cloned.1.call-done = bf16[32,1024]{1,0:T(8,128)(2,1)} async-done(((bf16[512,1024]{1,0:T(8,128)(2,1)}), bf16[32,1024]{1,0:T(8,128)(2,1)}) %reduce-scatter.4.cloned.1.call-update) | async-done | bytes 65552
  717.1 4.6 copy.58
  (224 shorter events, 199.0 us)
Async XLA Ops:
  11.2 57.8 %all-to-all-start.1 = ((bf16[128,16,512]{0,2,1:T(8,128)(2,1)}), bf16[128,16,512]{0,2,1:T(8,128)(2,1)S(1)}, u32[]{:S(2)}, u32[]{:S(2)}) async-start(bf16[128,16,512]{0,2,1:T(8,128)(2,1)} %bitcast.74), calls=%async_computation.1 | async-start | bytes 4194304 | tf_op jit(solution)/shard_map/all_to_all | solution.py:98
  19.8 64.1 %all-gather.5.cloned.1.call-start = ((), (), s32[]{:S(2)}) async-start(), calls=%async_computation.5 | async-start | bytes 1114112 | tf_op jit(solution)/shard_map/all_gather | solution.py:102
  20.6 137.6 %all-gather.3.cloned.1.call-start = ((), (), s32[]{:S(2)}) async-start(), calls=%async_computation.4 | async-start | bytes 2506752 | tf_op jit(solution)/shard_map/all_gather | solution.py:100
  69.0 1.4 copy-start
  69.0 6.0 copy-start.4
  70.4 104.0 %all-to-all-start = ((bf16[128,16,768]{0,2,1:T(8,128)(2,1)}), bf16[128,16,768]{0,2,1:T(8,128)(2,1)S(1)}, u32[]{:S(2)}, u32[]{:S(2)}) async-start(bf16[128,16,768]{0,2,1:T(8,128)(2,1)} %bitcast.7), calls=%async_computation | async-start | bytes 6291456 | tf_op jit(solution)/shard_map/all_to_all | solution.py:97
  168.9 3.4 slice-start
  168.9 3.5 copy-start.1
  460.6 253.7 %all-to-all-start.2 = ((bf16[16,128,768]{2,1,0:T(8,128)(2,1)}), bf16[16,128,768]{2,1,0:T(8,128)(2,1)S(1)}, u32[]{:S(2)}, u32[]{:S(2)}) async-start(bf16[16,128,768]{2,1,0:T(8,128)(2,1)} %copy.56), calls=%async_computation.2 | async-start | bytes 6291456 | tf_op jit(solution)/shard_map/all_to_all | solution.py:124
  466.7 163.7 %all-reduce.5.cloned.1.call-start = ((), (), s32[]{:S(2)}) async-start(), calls=%async_computation.6 | async-start | bytes 4718592 | tf_op jit(solution)/shard_map/psum | solution.py:139
  473.7 1.2 copy-start.3
  474.3 3.0 copy-start.2
  479.0 233.5 %reduce-scatter.4.cloned.1.call-start = ((), (), s32[]{:S(2)}) async-start(), calls=%async_computation.7 | async-start | bytes 1114112
Sparse Core Ops, SparseCore 0:
  23.1 48.6 all-gather.4
  73.5 84.6 all-gather.2
  479.2 151.1 all-reduce.4
  633.7 78.7 reduce-scatter.3
where the time goes:
time: 733 us; the launch traced here: 728 us
  waiting for transfers between devices  342 us (47%)
  matrix products  237 us (32%)
  local copies, waits for them, and re-layouts  94.5 us (13%)
  starting transfers between devices  19.7 us (3%)
  between operations  13.9 us (2%)
  loops' own time  11.1 us (2%)
  other arithmetic  10.1 us (1%)
    psum x1, waiting for transfers between devices, local(): lax.psum(head_terms.astype(jnp.bfloat16), 'head').astype(jnp.float32)  143 us
    unnamed x5, waiting for transfers between devices  81.9 us
    all_gather x1, waiting for transfers between devices, local(): latents = lax.all_gather(latent, 'head', axis=0, tiled=True)  74.2 us
    dot_general x16, matrix products, one_block(): jnp.einsum('hqk,qhd->khd', probs_low, out_rows, preferred_element_type=jn...  52.8 us
    dot_general x16, matrix products, one_block(): jnp.einsum('hqk,qhd->khd', dscore_low, query_rows, preferred_element_type...  49.7 us
    all_to_all x1, waiting for transfers between devices, local(): lax.all_to_all(d_attn, 'head', split_axis=1, concat_axis=0, tiled=True)  43.1 us
    dot_general x16, matrix products, one_block(): jnp.einsum('hqk,khd->qhd', dscore_low, key_rows, preferred_element_type=j...  34.8 us
    dot_general x16, matrix products, one_block(): jnp.einsum('hqk,khd->qhd', probs_low, value_rows, preferred_element_type=...  34.8 us
  transfers between devices with their start and end apart: 7, of which 4 were waited for; matrix products, arithmetic and copies ran while one was open for 7% of the time, Pallas kernels for 0%

commit v1 on v0

--- a/solution.py
+++ b/solution.py
@@ -11,6 +11,10 @@
 DOC_MAX = 384
 QB = 128
 masked_score = -1e30
+
+
+def answer_side(arr, which_axis):
+    return jnp.sum(lax.all_gather(arr, which_axis), axis=0)
 
 
 def document_index(lengths_row, count):
@@ -136,7 +140,7 @@
         grad_kv, whole_weight, (((1,), (1,)), ((), ())), preferred_element_type=jnp.float32
     )
     head_terms = jnp.concatenate([grad_compressed, jnp.sum(grad_keys[:, :, NOPE:], axis=1)], axis=1)
-    summed = lax.psum(head_terms.astype(jnp.bfloat16), "head").astype(jnp.float32)
+    summed = answer_side(head_terms.astype(jnp.bfloat16), which_axis="head").astype(jnp.float32)
     grad_latent = lax.dynamic_slice_in_dim(
         summed, lax.axis_index("head") * own_tokens, own_tokens, 0
     )

time: 733 us -> 768 us (1.048)
  waiting for transfers between devices: 342 us -> 365 us
  other arithmetic: 10.1 us -> 22.3 us
    all_gather x0 -> x1, waiting for transfers between devices: none -> 177 us  [answer_side(): return jnp.sum(lax.all_gather(arr, which_axis), axis=0)]
    psum x1 -> x0, waiting for transfers between devices: 143 us -> none  [local(): lax.psum(head_terms.astype(jnp.bfloat16), 'head').astype(jnp.float32)]
    unnamed x5, waiting for transfers between devices: 81.9 us -> 61.8 us
    reduce_sum x0 -> x1, other arithmetic: none -> 13 us  [answer_side(): return jnp.sum(lax.all_gather(arr, which_axis), axis=0)]
    all_to_all x1, waiting for transfers between devices: 0.01 us -> 9.61 us  [local(): lax.all_to_all(grad_queries, 'head', split_axis=0, concat_axis=1, tiled=T...]
    unnamed x17 -> x19, local copies, waits for them, and re-layouts: 23.4 us -> 24 us
  transfers between devices with their start and end apart: 7 -> 7, of which waited for: 4 -> 5; matrix products, arithmetic and copies ran while one was open for 7% -> 7% of each run, Pallas kernels for 0% -> 0%
where the time goes in v1:
time: 768 us; the launch traced here: 762 us
  waiting for transfers between devices  365 us (48%)
  matrix products  235 us (31%)
  local copies, waits for them, and re-layouts  95.2 us (12%)
  other arithmetic  22.3 us (3%)
  starting transfers between devices  19.5 us (3%)
  between operations  13.9 us (2%)
  loops' own time  11.1 us (1%)
    all_gather x1, waiting for transfers between devices, answer_side(): return jnp.sum(lax.all_gather(arr, which_axis), axis=0)  177 us
    all_gather x1, waiting for transfers between devices, local(): latents = lax.all_gather(latent, 'head', axis=0, tiled=True)  74.2 us
    unnamed x5, waiting for transfers between devices  61.8 us
    dot_general x16, matrix products, one_block(): jnp.einsum('hqk,qhd->khd', probs_low, out_rows, preferred_element_type=jn...  52.8 us
    dot_general x16, matrix products, one_block(): jnp.einsum('hqk,qhd->khd', dscore_low, query_rows, preferred_element_type...  49.5 us
    all_to_all x1, waiting for transfers between devices, local(): lax.all_to_all(d_attn, 'head', split_axis=1, concat_axis=0, tiled=True)  43.1 us
    dot_general x16, matrix products, one_block(): jnp.einsum('hqk,khd->qhd', dscore_low, key_rows, preferred_element_type=j...  35 us
    dot_general x16, matrix products, one_block(): jnp.einsum('hqk,khd->qhd', probs_low, value_rows, preferred_element_type=...  34.7 us
  transfers between devices with their start and end apart: 7, of which 5 were waited for; matrix products, arithmetic and copies ran while one was open for 7% of the time, Pallas kernels for 0%

profile of v1, /device:TPU:2, one launch (start us, length us, event | category | flops | bytes accessed | tf_op | source)
XLA Modules:
  0.0 762.4 jit_solution(7429441355461717063)
XLA Ops:
  7.2 4.1 copy.52
  11.2 8.6 %all-to-all-start.1 = ((bf16[128,16,512]{0,2,1:T(8,128)(2,1)}), bf16[128,16,512]{0,2,1:T(8,128)(2,1)S(1)}, u32[]{:S(2)}, u32[]{:S(2)}) async-start(bf16[128,16,512]{0,2,1:T(8,128)(2,1)} %bitcast.79), calls=%async_computation.1 | async-start | bytes 4194304 | tf_op jit(solution)/shard_map/all_to_all | solution.py:102
  21.3 4.6 copy.50
  25.9 43.1 %all-to-all-done.1 = bf16[128,16,512]{0,2,1:T(8,128)(2,1)S(1)} async-done(((bf16[128,16,512]{0,2,1:T(8,128)(2,1)}), bf16[128,16,512]{0,2,1:T(8,128)(2,1)S(1)}, u32[]{:S(2)}, u32[]{:S(2)}) %all-to-all-start.1) | async-done | bytes 2097184 | tf_op jit(solution)/shard_map/all_to_all | solution.py:102
  70.4 4.7 all-to-all-start
  75.4 4.3 copy.53
  79.8 4.2 reshape.148
  84.0 74.2 %all-gather.4.cloned.1.call-done = bf16[2048,576]{0,1:T(8,128)(2,1)} async-done(((bf16[128,576]{0,1:T(8,128)(2,1)}), bf16[2048,576]{0,1:T(8,128)(2,1)}) %all-gather.4.cloned.1.call-update) | async-done | bytes 2359312 | tf_op jit(solution)/shard_map/all_gather | solution.py:104
  158.1 4.2 convolution_convert_fusion
  164.9 4.0 copy.66
  168.9 3.4 concatenate.34
  174.4 3.7 copy.51
  178.1 5.8 reshape.144
  186.5 3.5 broadcast_in_dim.54
  189.9 265.8 %while.16 = (s32[]{:T(128)}, f32[2432,4,192]{0,2,1:T(8,128)}, f32[2432,4,128]{0,2,1:T(8,128)}, bf16[16,128,4,192]{1,3,2,0:T(8,128)(2,1)}, s32[16]{0:T(128)S(1)},...) while((s32[]{:T(128)}, f32[2432,4,192]{0,2,1:T(8,128)}, ...), condition=%wide.region_6.7_spmd, body=%wide.region_2.6_spmd.sunk | while | flops 711002240 | bytes 15294286 | solution.py:88
  200.2 3.3 fusion.129
  203.5 3.1 fusion.128
  216.8 3.3 fusion.129
  220.1 3.1 fusion.128
  233.5 3.3 fusion.129
  236.8 3.1 fusion.128
  250.1 3.3 fusion.129
  266.7 3.3 fusion.129
  270.0 3.1 fusion.128
  283.3 3.3 fusion.129
  299.9 3.3 fusion.129
  316.5 3.3 fusion.129
  333.1 3.3 fusion.129
  349.7 3.3 fusion.129
  353.0 3.1 fusion.128
  366.3 3.3 fusion.129
  382.9 3.3 fusion.129
  386.2 3.1 fusion.128
  399.5 3.3 fusion.129
  402.8 3.1 fusion.128
  416.1 3.3 fusion.129
  419.4 3.1 fusion.128
  432.7 3.3 fusion.129
  449.3 3.3 fusion.129
  452.6 3.1 fusion.128
  469.0 4.5 fusion.61
  475.3 4.7 copy.56
  480.0 6.1 all-to-all-start.2
  486.1 60.4 %reduce-scatter.4.cloned.1.call-done = bf16[32,1024]{1,0:T(8,128)(2,1)} async-done(((bf16[512,1024]{1,0:T(8,128)(2,1)}), bf16[32,1024]{1,0:T(8,128)(2,1)}) %reduce-scatter.4.cloned.1.call-update) | async-done | bytes 65552
  548.3 9.6 %all-to-all-done.2 = bf16[16,128,768]{2,1,0:T(8,128)(2,1)S(1)} async-done(((bf16[16,128,768]{2,1,0:T(8,128)(2,1)}), bf16[16,128,768]{2,1,0:T(8,128)(2,1)S(1)}, u32[]{:S(2)}, u32[]{:S(2)}) %all-to-all-start.2) | async-done | bytes 3145760 | tf_op jit(solution)/shard_map/all_to_all | solution.py:128
  560.7 4.7 copy.58
  565.4 176.6 %all-gather.8.cloned.1.call-done = bf16[16,2048,576]{1,2,0:T(8,128)(2,1)} async-done(((bf16[1,2048,576]{1,2,0:T(8,128)(2,1)}), bf16[16,2048,576]{1,2,0:T(8,128)(2,1)}) %all-gather.8.cloned.1.call-update) | async-done | bytes 37748752 | tf_op jit(solution)/shard_map/all_gather | solution.py:17
  742.0 13.0 %reduce_sum.56 = bf16[2048,576]{0,1:T(8,128)(2,1)S(1)} reduce(bf16[16,2048,576]{1,2,0:T(8,128)(2,1)} %all-gather.8.cloned.1.call-done, bf16[]{:T(256)} %constant.84.clone.1), dimensions={0}, to_apply=%region_8.9 | reduce | flops 17694720 | bytes 40108032 | tf_op jit(solution)/shard_map/reduce_sum | solution.py:17
  (227 shorter events, 204.6 us)
Async XLA Ops:
  11.2 57.8 %all-to-all-start.1 = ((bf16[128,16,512]{0,2,1:T(8,128)(2,1)}), bf16[128,16,512]{0,2,1:T(8,128)(2,1)S(1)}, u32[]{:S(2)}, u32[]{:S(2)}) async-start(bf16[128,16,512]{0,2,1:T(8,128)(2,1)} %bitcast.79), calls=%async_computation.1 | async-start | bytes 4194304 | tf_op jit(solution)/shard_map/all_to_all | solution.py:102
  19.8 64.1 %all-gather.6.cloned.1.call-start = ((), (), s32[]{:S(2)}) async-start(), calls=%async_computation.5 | async-start | bytes 1114112 | tf_op jit(solution)/shard_map/all_gather | solution.py:106
  20.6 137.6 %all-gather.4.cloned.1.call-start = ((), (), s32[]{:S(2)}) async-start(), calls=%async_computation.4 | async-start | bytes 2506752 | tf_op jit(solution)/shard_map/all_gather | solution.py:104
  69.0 1.4 copy-start
  69.0 6.1 copy-start.5
  70.4 104.0 %all-to-all-start = ((bf16[128,16,768]{0,2,1:T(8,128)(2,1)}), bf16[128,16,768]{0,2,1:T(8,128)(2,1)S(1)}, u32[]{:S(2)}, u32[]{:S(2)}) async-start(bf16[128,16,768]{0,2,1:T(8,128)(2,1)} %bitcast.7), calls=%async_computation | async-start | bytes 6291456 | tf_op jit(solution)/shard_map/all_to_all | solution.py:101
  75.1 471.4 %reduce-scatter.4.cloned.1.call-start = ((), (), s32[]{:S(2)}) async-start(), calls=%async_computation.7 | async-start | bytes 1114112
  168.9 3.4 slice-start
  168.9 3.5 copy-start.1
  460.7 2.7 copy-start.3
  461.3 2.1 copy-start.2
  465.8 3.2 copy-start.4
  467.2 274.9 %all-gather.8.cloned.1.call-start = ((), (), s32[]{:S(2)}) async-start(), calls=%async_computation.6 | async-start | bytes 40108032 | tf_op jit(solution)/shard_map/all_gather | solution.py:17
  480.0 77.9 %all-to-all-start.2 = ((bf16[16,128,768]{2,1,0:T(8,128)(2,1)}), bf16[16,128,768]{2,1,0:T(8,128)(2,1)S(1)}, u32[]{:S(2)}, u32[]{:S(2)}) async-start(bf16[16,128,768]{2,1,0:T(8,128)(2,1)} %copy.56), calls=%async_computation.2 | async-start | bytes 6291456 | tf_op jit(solution)/shard_map/all_to_all | solution.py:128
Sparse Core Ops, SparseCore 0:
  23.1 48.6 all-gather.5
  73.5 84.6 all-gather.3
  467.3 79.1 reduce-scatter.3
  548.2 193.8 all-gather.7
